TPU v7x, 512 devices: a whole 4x8x8 slice. The times are simulated.
512 devices in a mesh: grp: 16 (over z_lo, x), blk: 32 (over y, z_hi, core).
Axes of the slice: x: 4, y: 8, z: 8 (z_hi: 2, z_lo: 4; z = z_hi * 4 + z_lo), core: 2. Of those that a mesh axis runs over, the one named last changes fastest.
Arguments:
- queries: bfloat16 [65536, 4096], P(('grp', 'blk')), may hold values from -4 to 4
- passages: bfloat16 [65536, 4096], P(('grp', 'blk')), may hold values from -1 to 1
- hard_index: int32 [65536, 3], P(('grp', 'blk')), may hold values from 0 to 65535, as said below
- weights: float32 [65536], P(('grp', 'blk')), may hold values from 0.5 to 2
Outputs:
- loss_rows: float32 [65536], P(('grp', 'blk'))
- grad_queries: bfloat16 [65536, 4096], P(('grp', 'blk'))
- grad_passages: bfloat16 [65536, 4096], P(('grp', 'blk'))
Inputs may be any that keep to these rules, and one draw needn't show every extreme that they name: `hard_index`: the three entries of query i name passages of the block at the same index of blk as query i in three different groups, none its own; among the queries of one device at most 26 entries name one group, and in every device exactly 26 entries name some group.
All inputs are finite; a program needn't handle non-finite values.
Results may differ from a plain program's by a relative error of at most 0.0065.
Values may be sent and summed in bfloat16 or wider, within the bound.
A program may use at most 64 MiB of HBM per device.

v0:
```python
import jax
import jax.numpy as jnp
from jax import lax
from jax.sharding import PartitionSpec as P

WINDOW = 4


inv_temp = 50.0


def from_behind(array, axis, by):
    peers = lax.axis_size(axis)
    return lax.ppermute(array, axis, [(i, (i + by) % peers) for i in range(peers)])


def rows_times(left, right):
    return lax.dot_general(
        left, right, (((1,), (1,)), ((), ())), preferred_element_type=jnp.float32
    )


def columns_times(left, right):
    return lax.dot_general(
        left, right, (((0,), (0,)), ((), ())), preferred_element_type=jnp.float32
    )


def per_device(queries, passages, hard_index, weights):
    row_count, feature_width = queries.shape
    groups = lax.axis_size("grp")
    loop_size = lax.axis_size("blk")
    group_rows = loop_size * row_count
    capacity = max(2, (3 * row_count + groups - 2) // (groups - 1))
    slot_total = groups * capacity
    flat_index = hard_index.T.reshape(-1)
    target_group = flat_index // group_rows
    wanted_row = flat_index % row_count
    one_hot = (target_group[:, None] == jnp.arange(groups)[None, :]).astype(jnp.int32)
    slot_index = jnp.sum((jnp.cumsum(one_hot, axis=0) - one_hot) * one_hot, axis=1)
    slot_flat = target_group * capacity + slot_index
    requests = (
        jnp.full((groups, capacity), -1, jnp.int32).at[target_group, slot_index].set(wanted_row)
    )
    incoming = lax.all_to_all(requests, "grp", split_axis=0, concat_axis=0, tiled=True)
    picked = jnp.take(passages, jnp.clip(incoming, 0, row_count - 1).reshape(-1), axis=0)
    picked = picked.reshape(groups, capacity, feature_width)
    returned = lax.all_to_all(picked, "grp", split_axis=0, concat_axis=0, tiled=True).reshape(
        slot_total, feature_width
    )
    select = (
        slot_flat.reshape(3, row_count)[:, :, None] == jnp.arange(slot_total)[None, None, :]
    ).astype(jnp.float32)
    window_blocks = [passages]
    current = passages
    for step in range(1, WINDOW):
        current = from_behind(current, "blk", -1)
        window_blocks.append(current)
    window = jnp.concatenate(window_blocks, axis=0)
    scores = inv_temp * rows_times(queries, window)
    slot_scores = inv_temp * rows_times(queries, returned)
    hard_scores = jnp.sum(select * slot_scores[None, :, :], axis=2).T
    largest = jnp.maximum(jnp.max(scores, axis=1), jnp.max(hard_scores, axis=1))
    summed = jnp.sum(jnp.exp(scores - largest[:, None]), axis=1) + jnp.sum(
        jnp.exp(hard_scores - largest[:, None]), axis=1
    )
    log_total = largest + jnp.log(summed)
    positive = jnp.diagonal(scores[:, :row_count])
    loss_rows = log_total - positive
    weight_col = weights[:, None]
    weighting = (weight_col * jnp.exp(scores - log_total[:, None])).astype(jnp.bfloat16)
    hard_weighting = (weight_col * jnp.exp(hard_scores - log_total[:, None])).astype(jnp.bfloat16)
    hard_matrix = jnp.sum(select * hard_weighting.T.astype(jnp.float32)[:, :, None], axis=0).astype(
        jnp.bfloat16
    )
    pulled = jnp.dot(weighting, window, preferred_element_type=jnp.float32)
    pulled = pulled + jnp.dot(hard_matrix, returned, preferred_element_type=jnp.float32)
    grad_queries = (inv_temp * (pulled - weight_col * passages.astype(jnp.float32))).astype(
        jnp.bfloat16
    )
    outgoing = (
        columns_times(hard_matrix, queries)
        .astype(jnp.bfloat16)
        .reshape(groups, capacity, feature_width)
    )
    arrived = lax.all_to_all(outgoing, "grp", split_axis=0, concat_axis=0, tiled=True)
    owner_match = (incoming.reshape(-1)[None, :] == jnp.arange(row_count)[:, None]).astype(
        jnp.bfloat16
    )
    hard_sum = jnp.dot(
        owner_match, arrived.reshape(slot_total, feature_width), preferred_element_type=jnp.float32
    )
    carried = columns_times(weighting[:, (WINDOW - 1) * row_count :], queries)
    for step in range(WINDOW - 2, -1, -1):
        carried = from_behind(carried.astype(jnp.bfloat16), "blk", 1).astype(carried.dtype)
        coef_block = weighting[:, step * row_count : (step + 1) * row_count]
        carried = carried + columns_times(coef_block, queries)
    in_group = carried
    in_group = in_group - weight_col * queries.astype(jnp.float32)
    grad_passages = (inv_temp * (in_group + hard_sum)).astype(jnp.bfloat16)
    return (loss_rows, grad_queries, grad_passages)


def solution(mesh):
    in_specs = (
        P(("grp", "blk"), None),
        P(("grp", "blk"), None),
        P(("grp", "blk"), None),
        P(("grp", "blk")),
    )
    out_specs = (P(("grp", "blk")), P(("grp", "blk"), None), P(("grp", "blk"), None))
    return jax.shard_map(
        per_device, mesh=mesh, in_specs=in_specs, out_specs=out_specs, check_vma=False
    )
```

profile of v0, /device:TPU:152, one launch (start us, length us, event | category | flops | bytes accessed | tf_op | source)
XLA Modules:
  0.0 429.6 jit_solution(12030488142178340690)
XLA Ops:
  0.6 0.0 copy-start
  0.6 0.8 add_select_fusion
  1.4 0.7 add_select_fusion.2
  2.1 0.9 reduce-window.6
  3.0 0.2 slice_reduce_fusion
  3.2 0.1 fusion.20
  3.3 0.7 fusion.29
  4.1 20.1 %scatter_fusion = s32[16,26]{1,0:T(8,128)S(1)} fusion(s32[16,26]{1,0:T(8,128)S(1)} %broadcast_in_dim.14, s32[384]{0:T(512)S(1)} %fusion.29, s32[384]{0:T(512)S(1)} %get-tuple-element.8), kind=kCustom, calls=%fused_computation.2 | custom fusion | bytes 7680 | tf_op jit(solution)/shard_map/scatter | solution.py:43
  24.1 13.9 %all_to_all.22 = s32[16,1,26]{2,1,0:T(1,128)S(1)} all-to-all(s32[16,1,26]{2,1,0:T(1,128)S(1)} %bitcast.101), channel_id=1, replica_groups=mesh['grp'=16,'blk'=32] {'grp'}, dimensions={0} | all-to-all | bytes 3328 | tf_op jit(solution)/shard_map/all_to_all | solution.py:45
  38.1 0.5 broadcast.299
  38.6 0.7 fusion.32
  39.3 0.1 min.18
  39.4 0.0 copy-done
  39.4 4.1 gather_fusion
  43.5 4.9 %gather.11 = bf16[16,26,4096]{2,1,0:T(8,128)(2,1)} reshape(bf16[416,4096]{1,0:T(8,128)(2,1)} %gather_fusion) | data formatting | bytes 6815744 | tf_op jit(solution)/shard_map/jit(_take)/gather | solution.py:46
  48.4 4.6 %broadcast_select_fusion = bf16[16,26,4096]{2,1,0:T(8,128)(2,1)} fusion(bf16[16,26,4096]{2,1,0:T(8,128)(2,1)} %gather.11, pred[16,26]{1,0:T(8,128)(4,1)S(1)} %compare_and_fusion), kind=kLoop, calls=%fused_computation.9 | loop fusion | flops 1703936 | bytes 6816160 | tf_op jit(solution)/shard_map/jit(_take)/select_n | solution.py:46
  53.0 6.8 %all-to-all-start.1 = ((bf16[16,26,4096]{2,1,0:T(8,128)(2,1)}), bf16[16,26,4096]{2,1,0:T(8,128)(2,1)}, u32[]{:S(2)}, u32[]{:S(2)}) async-start(bf16[16,26,4096]{2,1,0:T(8,128)(2,1)} %broadcast_select_fusion), calls=%async_computation.1 | async-start | bytes 8388608 | tf_op jit(solution)/shard_map/all_to_all | solution.py:48
  59.9 5.8 %collective-permute-start = (bf16[128,4096]{1,0:T(8,128)(2,1)S(1)}, bf16[128,4096]{1,0:T(8,128)(2,1)S(1)}, u32[]{:S(2)}, u32[]{:S(2)}) collective-permute-start(bf16[128,4096]{1,0:T(8,128)(2,1)S(1)} %copy-done), channel_id=1, source_target_pairs={{0,31},{1,0},{2,1},{3,2},{4,3},{5,4},{6,5},{7,6},{8,7},{9,8},{10,9... | collective-permute-start | bytes 3145736 | tf_op jit(solution)/shard_map/ppermute | solution.py:14
  65.7 24.2 %collective-permute-done = bf16[128,4096]{1,0:T(8,128)(2,1)S(1)} collective-permute-done((bf16[128,4096]{1,0:T(8,128)(2,1)S(1)}, bf16[128,4096]{1,0:T(8,128)(2,1)S(1)}, u32[]{:S(2)}, u32[]{:S(2)}) %collective-permute-start) | collective-permute-done | bytes 1048608 | tf_op jit(solution)/shard_map/ppermute | solution.py:14
  89.9 8.7 %collective-permute-start.1 = (bf16[128,4096]{1,0:T(8,128)(2,1)S(1)}, bf16[128,4096]{1,0:T(8,128)(2,1)S(1)}, u32[]{:S(2)}, u32[]{:S(2)}) collective-permute-start(bf16[128,4096]{1,0:T(8,128)(2,1)S(1)} %collective-permute-done), channel_id=1, source_target_pairs={{0,31},{1,0},{2,1},{3,2},{4,3},{5,4},{6,5},{7,6},{8,7},{9,8},{10,9... | collective-permute-start | bytes 3145736 | tf_op jit(solution)/shard_map/ppermute | solution.py:14
  98.6 0.0 copy-done.5
  98.6 0.1 constant_dynamic-update-slice_fusion.3
  98.7 0.0 copy-start.1
  98.7 23.1 %collective-permute-done.1 = bf16[128,4096]{1,0:T(8,128)(2,1)S(1)} collective-permute-done((bf16[128,4096]{1,0:T(8,128)(2,1)S(1)}, bf16[128,4096]{1,0:T(8,128)(2,1)S(1)}, u32[]{:S(2)}, u32[]{:S(2)}) %collective-permute-start.1) | collective-permute-done | bytes 1048608 | tf_op jit(solution)/shard_map/ppermute | solution.py:14
  121.8 6.6 %collective-permute-start.2 = (bf16[128,4096]{1,0:T(8,128)(2,1)S(1)}, bf16[128,4096]{1,0:T(8,128)(2,1)S(1)}, u32[]{:S(2)}, u32[]{:S(2)}) collective-permute-start(bf16[128,4096]{1,0:T(8,128)(2,1)S(1)} %collective-permute-done.1), channel_id=1, source_target_pairs={{0,31},{1,0},{2,1},{3,2},{4,3},{5,4},{6,5},{7,6},{8,7},{9,8},{10,9... | collective-permute-start | bytes 3145736 | tf_op jit(solution)/shard_map/ppermute | solution.py:14
  128.5 0.1 constant_dynamic-update-slice_fusion.2
  128.6 0.1 constant_dynamic-update-slice_fusion.1
  128.7 16.3 %collective-permute-done.2 = bf16[128,4096]{1,0:T(8,128)(2,1)S(1)} collective-permute-done((bf16[128,4096]{1,0:T(8,128)(2,1)S(1)}, bf16[128,4096]{1,0:T(8,128)(2,1)S(1)}, u32[]{:S(2)}, u32[]{:S(2)}) %collective-permute-start.2) | collective-permute-done | bytes 1048608 | tf_op jit(solution)/shard_map/ppermute | solution.py:14
  145.0 0.1 constant_dynamic-update-slice_fusion
  145.0 0.0 copy-start.3
  145.1 1.9 copy-done.3
  147.0 0.0 copy-done.1
  147.0 1.3 fusion.34
  148.3 1.3 gather_fusion.1
  149.5 87.4 %all-to-all-done.1 = bf16[16,26,4096]{2,1,0:T(8,128)(2,1)} async-done(((bf16[16,26,4096]{2,1,0:T(8,128)(2,1)}), bf16[16,26,4096]{2,1,0:T(8,128)(2,1)}, u32[]{:S(2)}, u32[]{:S(2)}) %all-to-all-start.1) | async-done | bytes 3407904 | tf_op jit(solution)/shard_map/all_to_all | solution.py:48
  236.9 4.9 %reshape.224 = bf16[416,4096]{1,0:T(8,128)(2,1)} reshape(bf16[16,26,4096]{2,1,0:T(8,128)(2,1)} %all-to-all-done.1) | data formatting | bytes 6815744 | tf_op jit(solution)/shard_map/reshape | solution.py:48
  241.9 3.0 fusion.3
  244.9 0.1 select_reduce_fusion.1
  245.0 0.1 exponential_reduce_fusion
  245.1 0.5 fusion.33
  245.7 0.1 select_reduce_fusion
  245.7 2.8 convolution_convert_fusion
  248.5 4.9 %reshape.225 = bf16[16,26,4096]{2,1,0:T(8,128)(2,1)} reshape(bf16[416,4096]{1,0:T(8,128)(2,1)} %convolution_convert_fusion) | data formatting | bytes 6815744 | tf_op jit(solution)/shard_map/reshape | solution.py:84
  253.5 7.1 %all-to-all-start.2 = ((bf16[16,26,4096]{2,1,0:T(8,128)(2,1)}), bf16[16,26,4096]{2,1,0:T(8,128)(2,1)}, u32[]{:S(2)}, u32[]{:S(2)}) async-start(bf16[16,26,4096]{2,1,0:T(8,128)(2,1)} %reshape.225), calls=%async_computation.2 | async-start | bytes 8388608 | tf_op jit(solution)/shard_map/all_to_all | solution.py:86
  260.6 0.1 multiply_convert_fusion.1
  260.6 0.4 convolution_convert_fusion.1
  261.1 1.9 collective-permute-start.3
  263.0 33.2 %collective-permute-done.3 = bf16[128,4096]{1,0:T(8,128)(2,1)S(1)} collective-permute-done((bf16[128,4096]{1,0:T(8,128)(2,1)S(1)}, bf16[128,4096]{1,0:T(8,128)(2,1)S(1)}, u32[]{:S(2)}, u32[]{:S(2)}) %collective-permute-start.3) | collective-permute-done | bytes 1048608 | tf_op jit(solution)/shard_map/ppermute | solution.py:14
  296.2 1.4 add_convert_fusion.1
  297.6 12.5 %collective-permute-start.4 = (bf16[128,4096]{1,0:T(8,128)(2,1)}, bf16[128,4096]{1,0:T(8,128)(2,1)}, u32[]{:S(2)}, u32[]{:S(2)}) collective-permute-start(bf16[128,4096]{1,0:T(8,128)(2,1)} %add_convert_fusion.1), channel_id=1, source_target_pairs={{0,1},{1,2},{2,3},{3,4},{4,5},{5,6},{6,7},{7,8},{8,9},{9,10},{10,1... | collective-permute-start | bytes 3145736 | tf_op jit(solution)/shard_map/ppermute | solution.py:14
  310.0 0.1 all_to_all.17
  310.1 0.4 fusion.11
  310.6 2.7 fusion.35
  313.3 0.0 copy-start.4
  313.3 15.4 %collective-permute-done.4 = bf16[128,4096]{1,0:T(8,128)(2,1)} collective-permute-done((bf16[128,4096]{1,0:T(8,128)(2,1)}, bf16[128,4096]{1,0:T(8,128)(2,1)}, u32[]{:S(2)}, u32[]{:S(2)}) %collective-permute-start.4) | collective-permute-done | bytes 1048608 | tf_op jit(solution)/shard_map/ppermute | solution.py:14
  328.7 2.5 add_convert_fusion
  331.2 3.3 collective-permute-start.5
  334.5 1.8 fusion.9
  336.3 2.1 fusion.2
  338.4 80.7 %all-to-all-done.2 = bf16[16,26,4096]{2,1,0:T(8,128)(2,1)} async-done(((bf16[16,26,4096]{2,1,0:T(8,128)(2,1)}), bf16[16,26,4096]{2,1,0:T(8,128)(2,1)}, u32[]{:S(2)}, u32[]{:S(2)}) %all-to-all-start.2) | async-done | bytes 3407904 | tf_op jit(solution)/shard_map/all_to_all | solution.py:86
  419.1 4.9 %reshape.226 = bf16[416,4096]{1,0:T(8,128)(2,1)} reshape(bf16[16,26,4096]{2,1,0:T(8,128)(2,1)} %all-to-all-done.2) | data formatting | bytes 6815744 | tf_op jit(solution)/shard_map/reshape | solution.py:91
  423.9 2.8 fusion.4
  426.8 0.0 collective-permute-done.5
  426.8 2.8 multiply_convert_fusion
  (19 shorter events, 0.2 us)
Async XLA Ops:
  0.6 38.8 %copy-start = (bf16[128,4096]{1,0:T(8,128)(2,1)S(1)}, bf16[128,4096]{1,0:T(8,128)(2,1)}, u32[]{:S(2)}) copy-start(bf16[128,4096]{1,0:T(8,128)(2,1)} %param.5) | copy-start | bytes 3145732
  53.0 45.6 %copy-start.5 = (s32[128,3]{0,1:T(4,128)S(1)}, s32[128,3]{0,1:T(4,128)}, u32[]{:S(2)}) copy-start(s32[128,3]{0,1:T(4,128)} %param.6) | copy-start | bytes 4612
  53.0 183.9 %all-to-all-start.1 = ((bf16[16,26,4096]{2,1,0:T(8,128)(2,1)}), bf16[16,26,4096]{2,1,0:T(8,128)(2,1)}, u32[]{:S(2)}, u32[]{:S(2)}) async-start(bf16[16,26,4096]{2,1,0:T(8,128)(2,1)} %broadcast_select_fusion), calls=%async_computation.1 | async-start | bytes 8388608 | tf_op jit(solution)/shard_map/all_to_all | solution.py:48
  59.9 30.0 %collective-permute-start = (bf16[128,4096]{1,0:T(8,128)(2,1)S(1)}, bf16[128,4096]{1,0:T(8,128)(2,1)S(1)}, u32[]{:S(2)}, u32[]{:S(2)}) collective-permute-start(bf16[128,4096]{1,0:T(8,128)(2,1)S(1)} %copy-done), channel_id=1, source_target_pairs={{0,31},{1,0},{2,1},{3,2},{4,3},{5,4},{6,5},{7,6},{8,7},{9,8},{10,9... | collective-permute-start | bytes 3145736 | tf_op jit(solution)/shard_map/ppermute | solution.py:14
  89.9 31.9 %collective-permute-start.1 = (bf16[128,4096]{1,0:T(8,128)(2,1)S(1)}, bf16[128,4096]{1,0:T(8,128)(2,1)S(1)}, u32[]{:S(2)}, u32[]{:S(2)}) collective-permute-start(bf16[128,4096]{1,0:T(8,128)(2,1)S(1)} %collective-permute-done), channel_id=1, source_target_pairs={{0,31},{1,0},{2,1},{3,2},{4,3},{5,4},{6,5},{7,6},{8,7},{9,8},{10,9... | collective-permute-start | bytes 3145736 | tf_op jit(solution)/shard_map/ppermute | solution.py:14
  98.7 48.3 %copy-start.1 = (bf16[128,4096]{1,0:T(8,128)(2,1)S(1)}, bf16[128,4096]{1,0:T(8,128)(2,1)}, u32[]{:S(2)}) copy-start(bf16[128,4096]{1,0:T(8,128)(2,1)} %param.4) | copy-start | bytes 3145732
  121.8 23.1 %collective-permute-start.2 = (bf16[128,4096]{1,0:T(8,128)(2,1)S(1)}, bf16[128,4096]{1,0:T(8,128)(2,1)S(1)}, u32[]{:S(2)}, u32[]{:S(2)}) collective-permute-start(bf16[128,4096]{1,0:T(8,128)(2,1)S(1)} %collective-permute-done.1), channel_id=1, source_target_pairs={{0,31},{1,0},{2,1},{3,2},{4,3},{5,4},{6,5},{7,6},{8,7},{9,8},{10,9... | collective-permute-start | bytes 3145736 | tf_op jit(solution)/shard_map/ppermute | solution.py:14
  145.0 1.9 copy-start.3
  241.9 3.8 copy-start.6
  253.5 165.6 %all-to-all-start.2 = ((bf16[16,26,4096]{2,1,0:T(8,128)(2,1)}), bf16[16,26,4096]{2,1,0:T(8,128)(2,1)}, u32[]{:S(2)}, u32[]{:S(2)}) async-start(bf16[16,26,4096]{2,1,0:T(8,128)(2,1)} %reshape.225), calls=%async_computation.2 | async-start | bytes 8388608 | tf_op jit(solution)/shard_map/all_to_all | solution.py:86
  261.1 35.1 %collective-permute-start.3 = (bf16[128,4096]{1,0:T(8,128)(2,1)S(1)}, bf16[128,4096]{1,0:T(8,128)(2,1)S(1)}, u32[]{:S(2)}, u32[]{:S(2)}) collective-permute-start(bf16[128,4096]{1,0:T(8,128)(2,1)S(1)} %convolution_convert_fusion.1), channel_id=1, source_target_pairs={{0,1},{1,2},{2,3},{3,4},{4,5},{5,6},{6,7},{7,8},{8,9},{9,10},{10,1... | collective-permute-start | bytes 3145736 | tf_op jit(solution)/shard_map/ppermute | solution.py:14
  297.6 31.2 %collective-permute-start.4 = (bf16[128,4096]{1,0:T(8,128)(2,1)}, bf16[128,4096]{1,0:T(8,128)(2,1)}, u32[]{:S(2)}, u32[]{:S(2)}) collective-permute-start(bf16[128,4096]{1,0:T(8,128)(2,1)} %add_convert_fusion.1), channel_id=1, source_target_pairs={{0,1},{1,2},{2,3},{3,4},{4,5},{5,6},{6,7},{7,8},{8,9},{9,10},{10,1... | collective-permute-start | bytes 3145736 | tf_op jit(solution)/shard_map/ppermute | solution.py:14
  313.3 23.1 %copy-start.4 = (bf16[512,4096]{1,0:T(8,128)(2,1)S(1)}, bf16[512,4096]{1,0:T(8,128)(2,1)}, u32[]{:S(2)}) copy-start(bf16[512,4096]{1,0:T(8,128)(2,1)} %copy-done.3) | copy-start | bytes 12582916
  331.2 95.6 %collective-permute-start.5 = (bf16[128,4096]{1,0:T(8,128)(2,1)}, bf16[128,4096]{1,0:T(8,128)(2,1)}, u32[]{:S(2)}, u32[]{:S(2)}) collective-permute-start(bf16[128,4096]{1,0:T(8,128)(2,1)} %add_convert_fusion), channel_id=1, source_target_pairs={{0,1},{1,2},{2,3},{3,4},{4,5},{5,6},{6,7},{7,8},{8,9},{9,10},{10,1... | collective-permute-start | bytes 3145736 | tf_op jit(solution)/shard_map/ppermute | solution.py:14
  423.9 2.8 copy-start.2
where the time goes:
time: 431 us; the launch traced here: 430 us
  waiting for transfers between devices  280 us (65%)
  starting transfers between devices  52.9 us (12%)
  local copies, waits for them, and re-layouts  48.2 us (11%)
  matrix products  18.7 us (4%)
  other arithmetic  14.7 us (3%)
  blocking collectives  13.9 us (3%)
    ppermute x6, waiting for transfers between devices, from_behind(): lax.ppermute(array, axis, [(i, (i + by) % peers) for i in range(peers)])  112 us
    all_to_all x1, waiting for transfers between devices, per_device(): lax.all_to_all(picked, 'grp', split_axis=0, concat_axis=0, tiled=True)  87.4 us
    all_to_all x1, waiting for transfers between devices, per_device(): lax.all_to_all(outgoing, 'grp', split_axis=0, concat_axis=0, tiled=True)  80.7 us
    ppermute x6, starting transfers between devices, from_behind(): lax.ppermute(array, axis, [(i, (i + by) % peers) for i in range(peers)])  38.9 us
    scatter x1, local copies, waits for them, and re-layouts, per_device(): jnp.full((groups, capacity), -1, jnp.int32).at[target_group, slot_index]  20.1 us
    all_to_all x1, blocking collectives, per_device(): lax.all_to_all(requests, 'grp', split_axis=0, concat_axis=0, tiled=True)  13.9 us
    gather x2, local copies, waits for them, and re-layouts, per_device(): jnp.take(passages, jnp.clip(incoming, 0, row_count - 1).reshape(-1), axis=0)  9.03 us
  transfers between devices with their start and end apart: 8, of which 7 were waited for; matrix products, arithmetic and copies ran while one was open for 5% of the time, Pallas kernels for 0%

commit v1 on v0

v1 whole, which is shorter than its diff:
```python
import functools

import jax
import jax.numpy as jnp
from jax import lax
from jax.experimental import pallas as pl
from jax.experimental.pallas import tpu as pltpu
from jax.sharding import PartitionSpec as P

MESH = pl.DeviceIdType.MESH
TEMP = 50.0
SLOTS = 32
NEG = -3.0e38
F32, BF16 = jnp.float32, jnp.bfloat16


def nt(a, b):
    return lax.dot_general(a, b, (((1,), (1,)), ((), ())), preferred_element_type=F32)


def tn(a, b):
    return lax.dot_general(a, b, (((0,), (0,)), ((), ())), preferred_element_type=F32)


def nn(a, b):
    return lax.dot_general(a, b, (((1,), (0,)), ((), ())), preferred_element_type=F32)


def kernel(
    NC, Y, q_hbm, p_hbm, rt, st, mc, mx, wcol, loss, gq_hbm, gp_hbm,
    col, bw, tr, xs, xr, rx, sc, acc, wts, mts, wtw, wtc, mtx, oq, op,
    ld_s, st_s, z_s, col_r, tr_r, own_s, win_s, bw_r, x_s, x_r,
    rx_s, rx_r, sc_s, sc_r, ww_s, ww_r, wc_s, wc_r, mt_s, mt_r,
):
    rows = 128
    dc = gq_hbm.shape[1] // NC
    g = lax.axis_index("grp")
    b = lax.axis_index("blk")
    p, x = g // 4, g % 4
    y, h, c = b // 4, (b // 2) % 2, b % 2
    z = h * 4 + p
    loop = 4 * Y
    m = p // 2
    outer = (p == 0) | (p == 3)

    def a(k):
        return k + m * (3 - 2 * k)

    def zdev(zz):
        zz = (zz + 8) % 8
        return ((zz % 4) * 4 + x, y * 4 + (zz // 4) * 2 + c)

    def ydev(yy, cc):
        return (g, ((yy + Y) % Y) * 4 + h * 2 + cc)

    def bdev(off):
        return (g, (b + off + loop) % loop)

    def xdev(xx, pp):
        return (pp * 4 + xx, b)

    z_in, z_out = zdev(z + 1 - 2 * m), zdev(z - 1 + 2 * m)

    def rcopy(src, dst, ssem, rsem, dev):
        return pltpu.make_async_remote_copy(
            src_ref=src, dst_ref=dst, send_sem=ssem, recv_sem=rsem, device_id=dev, device_id_type=MESH
        )

    def got(ref, rsem):
        rcopy(ref, ref, rsem, rsem, bdev(1)).wait_recv()

    def sent(ref, ssem):
        rcopy(ref, ref, ssem, ssem, bdev(1)).wait_send()

    barrier = pltpu.get_barrier_semaphore()

    def hello(dev):
        pl.semaphore_signal(barrier, inc=1, device_id=dev, device_id_type=MESH)

    for k in range(1, 16):
        hello(((g + k) % 16, b))
    for off in (1, 2, 3, 4):
        hello(bdev(off))
        hello(bdev(-off))
    hello(bdev(5 - 10 * c))

    @pl.when(outer)
    def _():
        hello(z_out)

    def load(src, i, cc):
        return pltpu.make_async_copy(
            src.at[:, pl.ds(pl.multiple_of(cc * dc, dc), dc)], col.at[p, cc, i], ld_s.at[i, cc]
        )

    def start_load(cc, carry):
        load(p_hbm, 0, cc).start()
        load(q_hbm, 1, cc).start()
        return carry

    lax.fori_loop(0, NC, start_load, 0)

    pl.semaphore_wait(barrier, 25 - ((p + 1) // 2) % 2)

    for dx in (1, 2, 3):
        xd = (x + dx) % 4
        rcopy(rt.at[:, xd], rx.at[:, x], rx_s.at[dx - 1], rx_r.at[x], xdev(xd, p)).start()
        pd = (p + dx) % 4
        rcopy(st.at[pd], sc.at[p], sc_s.at[dx - 1], sc_r.at[p], xdev(x, pd)).start()
    rx[:, x] = jnp.zeros((4, SLOTS, rows), BF16)
    sc[p] = st[p]

    def own(cc):
        load(p_hbm, 0, cc).wait()
        load(q_hbm, 1, cc).wait()
        src = col.at[p, cc]
        rcopy(src, col.at[p, cc], z_s.at[0, cc], col_r.at[p, cc], z_in).start()

        @pl.when(jnp.logical_not(outer))
        def _():
            rcopy(src, col.at[p, cc], z_s.at[1, cc], col_r.at[p, cc], z_out).start()

        pdst = 2 - 2 * c
        rcopy(col.at[p, cc, 0], bw.at[pdst, cc], own_s.at[0, cc], bw_r.at[pdst, cc], ydev(y - 1 + c, 1 - c)).start()
        qdst = 3 + 2 * c
        rcopy(col.at[p, cc, 1], bw.at[qdst, cc], own_s.at[1, cc], bw_r.at[qdst, cc], ydev(y + c, 1 - c)).start()

    def fwd_col(l, cc, k, dev):
        got(col.at[l, cc], col_r.at[l, cc])
        rcopy(col.at[l, cc], col.at[l, cc], z_s.at[k, cc], col_r.at[l, cc], dev).start()

    def to_win(src, cc, k, dev, hh):
        pi, qi = 1 + 5 * hh, 6 - 2 * hh
        rcopy(src.at[0], bw.at[pi, cc], z_s.at[k, cc], bw_r.at[pi, cc], dev).start()
        rcopy(src.at[1], bw.at[qi, cc], z_s.at[k + 1, cc], bw_r.at[qi, cc], dev).start()

    def hop12(cc):
        @pl.when(outer)
        def _():
            got(col.at[a(2), cc], col_r.at[a(2), cc])
            rcopy(col.at[a(2), cc], tr.at[cc], z_s.at[2, cc], tr_r.at[cc], z_out).start()

        @pl.when(jnp.logical_not(outer))
        def _():
            fwd_col(a(0), cc, 2, z_in)
            fwd_col(a(2), cc, 3, z_out)
            fwd_col(a(3), cc, 4, z_out)

    def hop3(cc):
        @pl.when(outer)
        def _():
            got(col.at[a(3), cc], col_r.at[a(3), cc])
            to_win(col.at[a(3), cc], cc, 3, z_out, 1 - h)
            got(tr.at[cc], tr_r.at[cc])
            to_win(tr.at[cc], cc, 5, z_in, h)
            got(col.at[a(1), cc], col_r.at[a(1), cc])

    def win(cc):
        wi = 1 + 3 * h
        got(bw.at[wi, cc], bw_r.at[wi, cc])
        d = h * (5 - 2 * c) + (1 - h) * 2 * c
        rcopy(bw.at[wi, cc], bw.at[d, cc], win_s.at[0, cc], bw_r.at[d, cc], ydev(y, 1 - c)).start()
        got(bw.at[6, cc], bw_r.at[6, cc])
        for c2 in (0, 1):
            d = h * (1 - c2 + c) + (1 - h) * (4 + c2 - c)
            rcopy(
                bw.at[6, cc], bw.at[d, cc], win_s.at[1 + c2, cc], bw_r.at[d, cc], ydev(y + 1 - 2 * h, c2)
            ).start()

    def pick(cc):
        for l in range(4):
            rows_p = nn(rx[l].reshape(4 * SLOTS, rows), col[l, cc, 0]).astype(BF16)
            xs[:, cc, 0, l * SLOTS : (l + 1) * SLOTS, :] = rows_p.reshape(4, SLOTS, dc)
            rows_q = nn(sc[l].reshape(4 * SLOTS, rows), col[l, cc, 1]).astype(BF16)
            xs[:, cc, 1, l * SLOTS : (l + 1) * SLOTS, :] = rows_q.reshape(4, SLOTS, dc)
        for dx in (2, 1, 3):
            xd = (x + dx) % 4
            rcopy(xs.at[xd, cc], xr.at[x, cc], x_s.at[dx - 1, cc], x_r.at[x, cc], xdev(xd, p)).start()

    own(0)
    own(1)
    for dx in (1, 2, 3):
        got(rx.at[:, (x + dx) % 4], rx_r.at[(x + dx) % 4])
        got(sc.at[(p + dx) % 4], sc_r.at[(p + dx) % 4])

    def step(t, carry):
        @pl.when(t < NC)
        def _():
            @pl.when(t + 2 < NC)
            def _():
                own(t + 2)

            hop12(t)

        @pl.when((t >= 1) & (t < NC + 1))
        def _():
            hop3(t - 1)
            pick(t - 1)

        @pl.when(t >= 2)
        def _():
            win(t - 2)

        return carry

    lax.fori_loop(0, NC + 2, step, 0)

    acc[...] = jnp.zeros_like(acc)

    def score(cc, carry):
        for i in (0, 2, 3, 5):
            got(bw.at[i, cc], bw_r.at[i, cc])
        got(bw.at[4 - 3 * h, cc], bw_r.at[4 - 3 * h, cc])
        for dx in (1, 2, 3):
            got(xr.at[(x + dx) % 4, cc], x_r.at[(x + dx) % 4, cc])
        q = col[p, cc, 1]
        acc[0] += nt(q, col[p, cc, 0])
        for s in range(3):
            acc[1 + s] += nt(q, bw[s, cc])
            acc[4 + s] += nt(q, col[(p + 1 + s) % 4, cc, 0])
            acc[7 + s] += nt(q, xr[(x + 1 + s) % 4, cc, 0])
        return carry

    lax.fori_loop(0, NC, score, 0)

    w = wcol[...]
    masks = [mc[(p + 1 + s) % 4] for s in range(3)] + [mx[(x + 1 + s) % 4] for s in range(3)]
    scores = [TEMP * acc[k] for k in range(4)]
    scores += [jnp.where(masks[k] > 0.5, TEMP * acc[4 + k], NEG) for k in range(6)]
    top = scores[0]
    for k in range(1, 10):
        top = jnp.maximum(top, scores[k])
    top = jnp.max(top, axis=1, keepdims=True)
    total = jnp.zeros((rows, rows), F32)
    for k in range(10):
        e = jnp.exp(scores[k] - top)
        total += e if k < 4 else jnp.where(masks[k - 4] > 0.5, e, 0.0)
    log_total = top + jnp.log(jnp.sum(total, axis=1, keepdims=True))
    ri = lax.broadcasted_iota(jnp.int32, (rows, rows), 0)
    ci = lax.broadcasted_iota(jnp.int32, (rows, rows), 1)
    loss[...] = jnp.sum(jnp.where(ri == ci, log_total - scores[0], 0.0), axis=0, keepdims=True)
    for k in range(10):
        e = w * jnp.exp(scores[k] - log_total)
        wts[k] = (e if k < 4 else jnp.where(masks[k - 4] > 0.5, e, 0.0)).astype(BF16)
    ones = jnp.ones((rows, rows), BF16)
    for s in range(3):
        xd = (x + 1 + s) % 4
        by_slot = tn(wts[7 + s], ones)
        mts[s] = (by_slot * rt[:, xd].reshape(rows, rows).astype(F32)).astype(BF16).reshape(4, SLOTS, rows)

    for s in range(3):
        rcopy(wts.at[1 + s], wtw.at[s], ww_s.at[s], ww_r.at[s], bdev(1 + s)).start()
        pd = (p + 1 + s) % 4
        rcopy(wts.at[4 + s], wtc.at[p], wc_s.at[s], wc_r.at[p], xdev(x, pd)).start()
        xd = (x + 1 + s) % 4
        for l in range(4):
            rcopy(mts.at[s, l], mtx.at[x, p], mt_s.at[s, l], mt_r.at[x, p], xdev(xd, l)).start()

    def store(src, dst, i, cc):
        return pltpu.make_async_copy(
            src.at[cc], dst.at[:, pl.ds(pl.multiple_of(cc * dc, dc), dc)], st_s.at[i, cc]
        )

    def queries(cc, carry):
        own_p = col[p, cc, 0]
        tot = nn(wts[0], own_p)
        for s in range(3):
            tot += nn(wts[1 + s], bw[s, cc])
            tot += nn(wts[4 + s], col[(p + 1 + s) % 4, cc, 0])
            tot += nn(wts[7 + s], xr[(x + 1 + s) % 4, cc, 0])
        oq[cc] = (TEMP * (tot - w * own_p.astype(F32))).astype(BF16)
        store(oq, gq_hbm, 0, cc).start()
        return carry

    lax.fori_loop(0, NC, queries, 0)

    for s in range(3):
        got(wtw.at[s], ww_r.at[s])
        pd, xd = (p + 1 + s) % 4, (x + 1 + s) % 4
        got(wtc.at[pd], wc_r.at[pd])
        for l in range(4):
            got(mtx.at[xd, l], mt_r.at[xd, l])

    def passages(cc, carry):
        own_q = col[p, cc, 1]
        tot = tn(wts[0], own_q)
        for s in range(3):
            tot += tn(wtw[s], bw[3 + s, cc])
            pd, xd = (p + 1 + s) % 4, (x + 1 + s) % 4
            tot += tn(wtc[pd], col[pd, cc, 1])
            tot += tn(mtx[xd].reshape(rows, rows), xr[xd, cc, 1])
        op[cc] = (TEMP * (tot - w * own_q.astype(F32))).astype(BF16)
        store(op, gp_hbm, 1, cc).start()
        return carry

    lax.fori_loop(0, NC, passages, 0)

    def drain(cc, carry):
        store(oq, gq_hbm, 0, cc).wait()
        store(op, gp_hbm, 1, cc).wait()
        sent(col.at[p, cc], z_s.at[0, cc])
        sent(col.at[p, cc, 0], own_s.at[0, cc])
        sent(col.at[p, cc, 1], own_s.at[1, cc])
        sent(col.at[p, cc], z_s.at[2, cc])
        for k in range(3):
            sent(bw.at[6, cc], win_s.at[k, cc])
            sent(xs.at[0, cc], x_s.at[k, cc])

        @pl.when(outer)
        def _():
            for k in (3, 4, 5, 6):
                sent(col.at[p, cc, 0], z_s.at[k, cc])

        @pl.when(jnp.logical_not(outer))
        def _():
            for k in (1, 3, 4):
                sent(col.at[p, cc], z_s.at[k, cc])

        return carry

    lax.fori_loop(0, NC, drain, 0)
    for s in range(3):
        sent(rt.at[:, 0], rx_s.at[s])
        sent(st.at[0], sc_s.at[s])
        sent(wts.at[1 + s], ww_s.at[s])
        sent(wts.at[4 + s], wc_s.at[s])
        for l in range(4):
            sent(mts.at[s, l], mt_s.at[s, l])


def index_tiles(hard_index, x, rows, loop):
    target = hard_index // (loop * rows)
    wanted = hard_index % rows
    hit = target[:, :, None] == jnp.arange(16)[None, None, :]
    named = jnp.any(hit, axis=1).astype(F32)
    row = jnp.sum(jnp.where(hit, wanted[:, :, None], 0), axis=1)
    before = (jnp.arange(rows)[:, None] > jnp.arange(rows)[None, :]).astype(F32)
    rank = jnp.dot(before, named, preferred_element_type=F32).astype(jnp.int32)
    rank = jnp.where(named > 0, rank, -1)
    picks = rank.T[:, None, :] == jnp.arange(SLOTS)[None, :, None]
    slot_row = jnp.max(jnp.where(picks, row.T[:, None, :], -1), axis=2)
    st = picks.astype(BF16).reshape(4, 4, SLOTS, rows)
    rt = (slot_row[:, :, None] == jnp.arange(rows)[None, None, :]).astype(BF16).reshape(4, 4, SLOTS, rows)
    lanes = jnp.arange(rows)
    rank4 = rank.reshape(rows, 4, 4).transpose(2, 0, 1)
    lane_rank = jnp.repeat(rank4, SLOTS, axis=2)
    mx = (lane_rank == (lanes % SLOTS)[None, None, :]).astype(F32)
    col_id = jnp.arange(4) * 4 + x
    mc = jnp.any(
        (target[None, :, :, None] == col_id[:, None, None, None]) & (wanted[None, :, :, None] == lanes), axis=2
    ).astype(F32)
    return rt, st, mc, mx


def per_device(NC, Y, queries, passages, hard_index, weights):
    rows, width = queries.shape
    loop = 4 * Y
    x = lax.axis_index("grp") % 4
    rt, st, mc, mx = index_tiles(hard_index, x, rows, loop)
    dc = width // NC
    dma = pltpu.SemaphoreType.DMA
    vmem = pl.BlockSpec(memory_space=pltpu.VMEM)
    hbm = pl.BlockSpec(memory_space=pl.ANY)
    loss, gq, gp = pl.pallas_call(
        functools.partial(kernel, NC, Y),
        out_shape=(
            jax.ShapeDtypeStruct((1, rows), F32),
            jax.ShapeDtypeStruct((rows, width), BF16),
            jax.ShapeDtypeStruct((rows, width), BF16),
        ),
        in_specs=[hbm, hbm, vmem, vmem, vmem, vmem, vmem],
        out_specs=(vmem, hbm, hbm),
        scratch_shapes=[
            pltpu.VMEM((4, NC, 2, rows, dc), BF16),
            pltpu.VMEM((7, NC, rows, dc), BF16),
            pltpu.VMEM((NC, 2, rows, dc), BF16),
            pltpu.VMEM((4, NC, 2, rows, dc), BF16),
            pltpu.VMEM((4, NC, 2, rows, dc), BF16),
            pltpu.VMEM((4, 4, SLOTS, rows), BF16),
            pltpu.VMEM((4, 4, SLOTS, rows), BF16),
            pltpu.VMEM((10, rows, rows), F32),
            pltpu.VMEM((10, rows, rows), BF16),
            pltpu.VMEM((3, 4, SLOTS, rows), BF16),
            pltpu.VMEM((3, rows, rows), BF16),
            pltpu.VMEM((4, rows, rows), BF16),
            pltpu.VMEM((4, 4, SLOTS, rows), BF16),
            pltpu.VMEM((NC, rows, dc), BF16),
            pltpu.VMEM((NC, rows, dc), BF16),
            dma((2, NC)),
            dma((2, NC)),
            dma((7, NC)),
            dma((4, NC)),
            dma((NC,)),
            dma((2, NC)),
            dma((3, NC)),
            dma((7, NC)),
            dma((3, NC)),
            dma((4, NC)),
            dma((3,)), dma((4,)),
            dma((3,)), dma((4,)),
            dma((3,)), dma((3,)),
            dma((3,)), dma((4,)),
            dma((3, 4)), dma((4, 4)),
        ],
        compiler_params=pltpu.CompilerParams(
            collective_id=0, has_side_effects=True, vmem_limit_bytes=60 * 1024 * 1024
        ),
    )(queries, passages, rt, st, mc, mx, weights[:, None])
    return loss.reshape(rows), gq, gp


def solution(mesh):
    in_specs = (
        P(("grp", "blk"), None),
        P(("grp", "blk"), None),
        P(("grp", "blk"), None),
        P(("grp", "blk")),
    )
    out_specs = (P(("grp", "blk")), P(("grp", "blk"), None), P(("grp", "blk"), None))
    chunks = 8
    return jax.shard_map(
        functools.partial(per_device, chunks, mesh.shape["blk"] // 4),
        mesh=mesh, in_specs=in_specs, out_specs=out_specs, check_vma=False,
    )
```

time: 431 us -> 205 us (0.48)
  the two profiles are of different devices: /device:TPU:152 before, /device:TPU:1 now
where the time goes in v1:
time: 205 us; the launch traced here: 204 us
  Pallas kernels  194 us (95%)
  local copies, waits for them, and re-layouts  6.44 us (3%)
  other arithmetic  3.1 us (2%)
    pallas_call x1, Pallas kernels, per_device(): pl.pallas_call(functools.partial(kernel, NC, Y), out_shape=(jax.ShapeDtyp...  194 us
    unnamed x11, local copies, waits for them, and re-layouts  5.56 us

profile of v1, /device:TPU:1, one launch (start us, length us, event | category | flops | bytes accessed | tf_op | source)
XLA Modules:
  0.0 204.4 jit_solution(17930406505598317061)
XLA Ops:
  0.7 0.0 copy-start.1
  0.7 0.7 copy-done.1
  1.4 0.1 broadcast_compare_fusion
  1.4 0.1 fusion
  1.6 0.3 select_reduce_fusion
  2.0 0.1 iota_compare_fusion.3
  2.1 0.0 copy-start.2
  2.1 0.3 and_reduce_fusion
  2.4 0.4 copy-done.2
  2.7 0.7 copy.22.wcol
  3.5 0.7 convert_element_type.29.mc
  4.2 0.1 copy.21
  4.4 0.7 compare_convert_fusion.mx
  5.1 0.8 fusion.1
  5.9 194.0 %shard_map.67 = (f32[1,128]{1,0:T(1,128)}, bf16[128,4096]{1,0:T(8,128)(2,1)}, bf16[128,4096]{1,0:T(8,128)(2,1)}) custom-call(bf16[128,4096]{1,0:T(8,128)(2,1)} %q_hbm.1, bf16[128,4096]{1,0:T(8,128)(2,1)} %p_hbm.1, bf16[4,4,32,128]{3,2,1,0:T(8,128)(2,1)} %get-tuple-element.11.rt, bf16[4,4,32,128]{3,2,1,0:T(8,128)(2,1)} %get-tuple-element.12.st, ...), custom_call_target="tpu_custom_call" | custom-call | tf_op jit(solution)/shard_map/pallas_call | solution.py:364
  199.8 0.0 copy-start.3
  199.9 0.7 copy-done.3
  200.5 0.5 copy.26
  201.0 0.0 copy-start
  201.0 2.4 %copy.27 = bf16[128,4096]{1,0:T(8,128)(2,1)} copy(bf16[128,4096]{1,0:T(8,128)(2,1)} %get-tuple-element.17) | data formatting | bytes 2097152
  203.4 0.0 copy-done
  203.4 1.0 copy.28
  (7 shorter events, 0.1 us)
Async XLA Ops:
  0.7 0.7 copy-start.1
  2.1 0.7 copy-start.2
  199.8 0.7 copy-start.3
  201.0 2.4 %copy-start = (bf16[128,4096]{1,0:T(8,128)(2,1)S(1)}, bf16[128,4096]{1,0:T(8,128)(2,1)}, u32[]{:S(2)}) copy-start(bf16[128,4096]{1,0:T(8,128)(2,1)} %get-tuple-element.18) | copy-start | bytes 3145732

commit v2 on v1

v2 whole, which is shorter than its diff:
```python
import functools

import jax
import jax.numpy as jnp
from jax import lax
from jax.experimental import pallas as pl
from jax.experimental.pallas import tpu as pltpu
from jax.sharding import PartitionSpec as P

MESH = pl.DeviceIdType.MESH
TEMP = 50.0
SLOTS = 32
LAG = 4
NEG = -3.0e38
F32, BF16 = jnp.float32, jnp.bfloat16


def nt(a, b):
    return lax.dot_general(a, b, (((1,), (1,)), ((), ())), preferred_element_type=F32)


def tn(a, b):
    return lax.dot_general(a, b, (((0,), (0,)), ((), ())), preferred_element_type=F32)


def nn(a, b):
    return lax.dot_general(a, b, (((1,), (0,)), ((), ())), preferred_element_type=F32)


def kernel(
    NC, Y, CAP, q_hbm, p_hbm, hidx, wrow, loss, gq_hbm, gp_hbm,
    col, bw, tr, xs, xr, ob, rt, st, rx, sc, rxo, pk, mx, wm, acc, wts, mts, wtw, mtx, oq, op,
    ld_s, st_s, z_s, col_r, tr_r, own_s, win_s, bw_r, x_s, x_r,
    rx_s, rx_r, sc_s, sc_r, ro_s, ro_r, ww_s, ww_r, mt_s, mt_r,
):
    rows = 128
    dc = gq_hbm.shape[1] // NC
    packed = 4 * CAP
    g = lax.axis_index("grp")
    b = lax.axis_index("blk")
    p, x = g // 4, g % 4
    y, h, c = b // 4, (b // 2) % 2, b % 2
    z = h * 4 + p
    loop = 4 * Y
    m = p // 2
    outer = (p == 0) | (p == 3)
    inner = jnp.logical_not(outer)

    def a(k):
        return k + m * (3 - 2 * k)

    def zdev(zz):
        zz = (zz + 8) % 8
        return ((zz % 4) * 4 + x, y * 4 + (zz // 4) * 2 + c)

    def ydev(yy, cc):
        return (g, ((yy + Y) % Y) * 4 + h * 2 + cc)

    def bdev(off):
        return (g, (b + off + loop) % loop)

    def xdev(xx, pp):
        return (pp * 4 + xx, b)

    z_in, z_out = zdev(z + 1 - 2 * m), zdev(z - 1 + 2 * m)

    def rcopy(src, dst, ssem, rsem, dev):
        return pltpu.make_async_remote_copy(
            src_ref=src, dst_ref=dst, send_sem=ssem, recv_sem=rsem, device_id=dev, device_id_type=MESH
        )

    def got(ref, rsem):
        rcopy(ref, ref, rsem, rsem, bdev(1)).wait_recv()

    def sent(ref, ssem):
        rcopy(ref, ref, ssem, ssem, bdev(1)).wait_send()

    barrier = pltpu.get_barrier_semaphore()

    def hello(dev):
        pl.semaphore_signal(barrier, inc=1, device_id=dev, device_id_type=MESH)

    for k in range(1, 16):
        hello(((g + k) % 16, b))
    for off in (1, 2, 3, 4):
        hello(bdev(off))
        hello(bdev(-off))
    hello(bdev(5 - 10 * c))

    @pl.when(outer)
    def _():
        hello(z_out)

    def load(src, i, cc):
        return pltpu.make_async_copy(
            src.at[:, pl.ds(pl.multiple_of(cc * dc, dc), dc)], col.at[p, cc, i], ld_s.at[i, cc]
        )

    def start_load(cc, carry):
        load(p_hbm, 0, cc).start()
        load(q_hbm, 1, cc).start()
        return carry

    lax.fori_loop(0, NC, start_load, 0)

    ri = lax.broadcasted_iota(jnp.int32, (rows, rows), 0)
    ci = lax.broadcasted_iota(jnp.int32, (rows, rows), 1)
    target = lax.div(hidx[...], jnp.full((3, rows), loop * rows, jnp.int32))
    wanted = lax.rem(hidx[...], jnp.full((3, rows), rows, jnp.int32)).astype(F32)
    gi = lax.broadcasted_iota(jnp.int32, (16, rows), 0)
    named = jnp.zeros((16, rows), F32)
    row = jnp.zeros((16, rows), F32)
    for k in range(3):
        hit = gi == target[k : k + 1]
        named += jnp.where(hit, 1.0, 0.0)
        row += jnp.where(hit, wanted[k : k + 1], 0.0)
    rank = nn(named.astype(BF16), jnp.where(ri < ci, 1.0, 0.0).astype(BF16))
    rank = jnp.where(named > 0.5, rank, -1.0).astype(jnp.int32)
    slot = lax.broadcasted_iota(jnp.int32, (SLOTS, rows), 0)
    lane = lax.broadcasted_iota(jnp.int32, (SLOTS, rows), 1).astype(F32)
    for k in range(16):
        pick = slot == rank[k : k + 1]
        st[k // 4, k % 4] = jnp.where(pick, 1.0, 0.0).astype(BF16)
        slot_row = jnp.max(jnp.where(pick, row[k : k + 1], -1.0), axis=1, keepdims=True)
        rt[k // 4, k % 4] = jnp.where(slot_row == lane, 1.0, 0.0).astype(BF16)

    @pl.when(outer)
    def _():
        def clear(cc, carry):
            col[a(1), cc, :, packed:, :] = jnp.zeros((2, rows - packed, dc), BF16)
            return carry

        lax.fori_loop(0, NC, clear, 0)

    pl.semaphore_wait(barrier, 25 - ((p + 1) // 2) % 2)

    def own(cc):
        load(p_hbm, 0, cc).wait()
        load(q_hbm, 1, cc).wait()
        rcopy(col.at[p, cc], col.at[p, cc], z_s.at[0, cc], col_r.at[p, cc], z_in).start()
        pdst = 2 - 2 * c
        rcopy(col.at[p, cc, 0], bw.at[pdst, cc], own_s.at[0, cc], bw_r.at[pdst, cc], ydev(y - 1 + c, 1 - c)).start()
        qdst = 3 + 2 * c
        rcopy(col.at[p, cc, 1], bw.at[qdst, cc], own_s.at[1, cc], bw_r.at[qdst, cc], ydev(y + c, 1 - c)).start()

    def own_out(cc):
        @pl.when(inner)
        def _():
            for i in range(2):
                ob[cc, i] = nn(pk[i], col[p, cc, i]).astype(BF16)
            rcopy(
                ob.at[cc, :, pl.ds(0, packed)], col.at[p, cc, :, pl.ds(0, packed)],
                z_s.at[1, cc], col_r.at[p, cc], z_out,
            ).start()

    own(0)
    own(1)

    @pl.when(outer)
    def _():
        for k in range(4):
            rcopy(rt.at[a(1), k], rxo.at[x], ro_s.at[k], ro_r.at[x], xdev(k, a(1))).start()

    for dx in (1, 2, 3):
        xd = (x + dx) % 4
        rcopy(rt.at[:, xd], rx.at[:, x], rx_s.at[dx - 1], rx_r.at[x], xdev(xd, p)).start()
        pd = (p + dx) % 4
        rcopy(st.at[pd], sc.at[p], sc_s.at[dx - 1], sc_r.at[p], xdev(x, pd)).start()
    rx[:, x] = rt[:, x]
    sc[p] = st[p]
    mtx[x, p] = jnp.zeros((SLOTS, rows), BF16)
    acc[...] = jnp.zeros_like(acc)
    wm[...] = jnp.broadcast_to(wrow[...], (rows, rows)).T
    for k in range(4):
        mx[k] = st[:, (x + k) % 4].reshape(rows, rows).astype(F32).T

    unpack = jnp.where((ri % SLOTS < CAP) & (ci == (ri // SLOTS) * CAP + ri % SLOTS), 1.0, 0.0).astype(BF16)

    @pl.when(inner)
    def _():
        for k in range(4):
            got(rxo.at[k], ro_r.at[k])
        pk[0] = tn(unpack, rxo[...].reshape(rows, rows)).astype(BF16)
        pk[1] = tn(unpack, st[a(0)].reshape(rows, rows)).astype(BF16)

    own_out(0)
    own_out(1)
    for dx in (1, 2, 3):
        got(rx.at[:, (x + dx) % 4], rx_r.at[(x + dx) % 4])
        got(sc.at[(p + dx) % 4], sc_r.at[(p + dx) % 4])

    @pl.when(outer)
    def _():
        rx[a(1)] = unpack.reshape(4, SLOTS, rows)
        sc[a(1)] = unpack.reshape(4, SLOTS, rows)

    def fwd_col(l, cc, k, dev):
        got(col.at[l, cc], col_r.at[l, cc])
        rcopy(col.at[l, cc], col.at[l, cc], z_s.at[k, cc], col_r.at[l, cc], dev).start()

    def to_win(src, cc, k, dev, hh):
        pi, qi = 1 + 5 * hh, 6 - 2 * hh
        rcopy(src.at[0], bw.at[pi, cc], z_s.at[k, cc], bw_r.at[pi, cc], dev).start()
        rcopy(src.at[1], bw.at[qi, cc], z_s.at[k + 1, cc], bw_r.at[qi, cc], dev).start()

    def hop12(cc):
        @pl.when(outer)
        def _():
            got(col.at[a(2), cc], col_r.at[a(2), cc])
            rcopy(col.at[a(2), cc], tr.at[cc], z_s.at[2, cc], tr_r.at[cc], z_out).start()

        @pl.when(inner)
        def _():
            fwd_col(a(0), cc, 2, z_in)
            fwd_col(a(2), cc, 3, z_out)
            fwd_col(a(3), cc, 4, z_out)

    def hop3(cc):
        @pl.when(outer)
        def _():
            got(col.at[a(3), cc], col_r.at[a(3), cc])
            to_win(col.at[a(3), cc], cc, 3, z_out, 1 - h)
            got(tr.at[cc], tr_r.at[cc])
            to_win(tr.at[cc], cc, 5, z_in, h)
            part = col.at[a(1), cc, :, pl.ds(0, packed)]
            got(part, col_r.at[a(1), cc])

    def win(cc):
        wi = 1 + 3 * h
        got(bw.at[wi, cc], bw_r.at[wi, cc])
        d = h * (5 - 2 * c) + (1 - h) * 2 * c
        rcopy(bw.at[wi, cc], bw.at[d, cc], win_s.at[0, cc], bw_r.at[d, cc], ydev(y, 1 - c)).start()
        got(bw.at[6, cc], bw_r.at[6, cc])
        for c2 in (0, 1):
            d = h * (1 - c2 + c) + (1 - h) * (4 + c2 - c)
            rcopy(
                bw.at[6, cc], bw.at[d, cc], win_s.at[1 + c2, cc], bw_r.at[d, cc], ydev(y + 1 - 2 * h, c2)
            ).start()

    def pick_rows(cc):
        for l in range(4):
            rows_p = nn(rx[l].reshape(4 * SLOTS, rows), col[l, cc, 0]).astype(BF16)
            xs[:, cc, 0, l * SLOTS : (l + 1) * SLOTS, :] = rows_p.reshape(4, SLOTS, dc)
            rows_q = nn(sc[l].reshape(4 * SLOTS, rows), col[l, cc, 1]).astype(BF16)
            xs[:, cc, 1, l * SLOTS : (l + 1) * SLOTS, :] = rows_q.reshape(4, SLOTS, dc)
        for dx in (2, 1, 3):
            xd = (x + dx) % 4
            rcopy(xs.at[xd, cc], xr.at[x, cc], x_s.at[dx - 1, cc], x_r.at[x, cc], xdev(xd, p)).start()

    def score(cc):
        for i in (0, 2, 3, 5):
            got(bw.at[i, cc], bw_r.at[i, cc])
        got(bw.at[4 - 3 * h, cc], bw_r.at[4 - 3 * h, cc])
        for dx in (1, 2, 3):
            got(xr.at[(x + dx) % 4, cc], x_r.at[(x + dx) % 4, cc])
        q = col[p, cc, 1]
        acc[0] += nt(q, col[p, cc, 0])
        acc[4] += nt(q, xs[x, cc, 0])
        for s in range(3):
            acc[1 + s] += nt(q, bw[s, cc])
            acc[5 + s] += nt(q, xr[(x + 1 + s) % 4, cc, 0])

    def step(t, carry):
        @pl.when(t + 2 < NC)
        def _():
            own(t + 2)
            own_out(t + 2)

        @pl.when(t < NC)
        def _():
            hop12(t)

        @pl.when((t >= 1) & (t < NC + 1))
        def _():
            hop3(t - 1)

        @pl.when((t >= 2) & (t < NC + 2))
        def _():
            win(t - 2)

        @pl.when((t >= 1) & (t < NC + 1))
        def _():
            pick_rows(t - 1)

        @pl.when(t >= LAG)
        def _():
            score(t - LAG)

        return carry

    lax.fori_loop(0, NC + LAG, step, 0)

    w = wm[...]
    scores = [TEMP * acc[k] for k in range(4)]
    scores += [jnp.where(mx[k] > 0.5, TEMP * acc[4 + k], NEG) for k in range(4)]
    top = scores[0]
    for k in range(1, 8):
        top = jnp.maximum(top, scores[k])
    top = jnp.max(top, axis=1, keepdims=True)
    total = jnp.zeros((rows, rows), F32)
    for k in range(8):
        e = jnp.exp(scores[k] - top)
        total += e if k < 4 else jnp.where(mx[k - 4] > 0.5, e, 0.0)
    log_total = top + jnp.log(jnp.sum(total, axis=1, keepdims=True))
    for k in range(8):
        e = w * jnp.exp(scores[k] - log_total)
        wts[k] = (e if k < 4 else jnp.where(mx[k - 4] > 0.5, e, 0.0)).astype(BF16)
    ones = jnp.ones((rows, rows), BF16)
    for k in range(4):
        by_slot = tn(wts[4 + k], ones)
        want = rt[:, (x + k) % 4].reshape(rows, rows).astype(F32)
        mts[k] = (by_slot * want).astype(BF16).reshape(4, SLOTS, rows)

    for s in range(3):
        rcopy(wts.at[1 + s], wtw.at[s], ww_s.at[s], ww_r.at[s], bdev(1 + s)).start()
        pd = (p + 1 + s) % 4
        rcopy(mts.at[0, pd], mtx.at[x, p], mt_s.at[0, pd], mt_r.at[x, p], xdev(x, pd)).start()
        xd = (x + 1 + s) % 4
        for l in range(4):
            rcopy(mts.at[1 + s, l], mtx.at[x, p], mt_s.at[1 + s, l], mt_r.at[x, p], xdev(xd, l)).start()

    loss[...] = jnp.sum(jnp.where(ri == ci, log_total - scores[0], 0.0), axis=0, keepdims=True)

    def store(src, dst, i, cc):
        return pltpu.make_async_copy(
            src.at[cc], dst.at[:, pl.ds(pl.multiple_of(cc * dc, dc), dc)], st_s.at[i, cc]
        )

    def queries(cc, carry):
        own_p = col[p, cc, 0]
        tot = nn(wts[0], own_p)
        tot += nn(wts[4], xs[x, cc, 0])
        for s in range(3):
            tot += nn(wts[1 + s], bw[s, cc])
            tot += nn(wts[5 + s], xr[(x + 1 + s) % 4, cc, 0])
        oq[cc] = (TEMP * (tot - wm[:, :1] * own_p.astype(F32))).astype(BF16)
        store(oq, gq_hbm, 0, cc).start()
        return carry

    lax.fori_loop(0, NC, queries, 0)

    for s in range(3):
        got(wtw.at[s], ww_r.at[s])
        pd, xd = (p + 1 + s) % 4, (x + 1 + s) % 4
        got(mtx.at[x, pd], mt_r.at[x, pd])
        for l in range(4):
            got(mtx.at[xd, l], mt_r.at[xd, l])

    def passages(cc, carry):
        own_q = col[p, cc, 1]
        tot = tn(wts[0], own_q)
        tot += tn(mtx[x].reshape(rows, rows), xs[x, cc, 1])
        for s in range(3):
            xd = (x + 1 + s) % 4
            tot += tn(wtw[s], bw[3 + s, cc])
            tot += tn(mtx[xd].reshape(rows, rows), xr[xd, cc, 1])
        op[cc] = (TEMP * (tot - wm[:, :1] * own_q.astype(F32))).astype(BF16)
        store(op, gp_hbm, 1, cc).start()
        return carry

    lax.fori_loop(0, NC, passages, 0)

    def drain(cc, carry):
        store(oq, gq_hbm, 0, cc).wait()
        store(op, gp_hbm, 1, cc).wait()
        sent(col.at[p, cc], z_s.at[0, cc])
        sent(col.at[p, cc, 0], own_s.at[0, cc])
        sent(col.at[p, cc, 1], own_s.at[1, cc])
        sent(col.at[p, cc], z_s.at[2, cc])
        for k in range(3):
            sent(bw.at[6, cc], win_s.at[k, cc])
            sent(xs.at[0, cc], x_s.at[k, cc])

        @pl.when(outer)
        def _():
            for k in (3, 4, 5, 6):
                sent(col.at[p, cc, 0], z_s.at[k, cc])

        @pl.when(inner)
        def _():
            sent(ob.at[cc, :, pl.ds(0, packed)], z_s.at[1, cc])
            for k in (3, 4):
                sent(col.at[p, cc], z_s.at[k, cc])

        return carry

    lax.fori_loop(0, NC, drain, 0)

    @pl.when(outer)
    def _():
        for k in range(4):
            sent(rt.at[0, 0], ro_s.at[k])

    for s in range(3):
        sent(rt.at[:, 0], rx_s.at[s])
        sent(st.at[0], sc_s.at[s])
        sent(wts.at[1 + s], ww_s.at[s])
        sent(mts.at[0, 0], mt_s.at[0, (p + 1 + s) % 4])
        for l in range(4):
            sent(mts.at[1 + s, l], mt_s.at[1 + s, l])


def per_device(NC, Y, queries, passages, hard_index, weights):
    rows, width = queries.shape
    cap = max(2, (3 * rows + 14) // 15)
    dc = width // NC
    dma = pltpu.SemaphoreType.DMA
    vmem = pl.BlockSpec(memory_space=pltpu.VMEM)
    hbm = pl.BlockSpec(memory_space=pl.ANY)
    loss, gq, gp = pl.pallas_call(
        functools.partial(kernel, NC, Y, cap),
        out_shape=(
            jax.ShapeDtypeStruct((1, rows), F32),
            jax.ShapeDtypeStruct((rows, width), BF16),
            jax.ShapeDtypeStruct((rows, width), BF16),
        ),
        in_specs=[hbm, hbm, vmem, vmem],
        out_specs=(vmem, hbm, hbm),
        scratch_shapes=[
            pltpu.VMEM((4, NC, 2, rows, dc), BF16),
            pltpu.VMEM((7, NC, rows, dc), BF16),
            pltpu.VMEM((NC, 2, rows, dc), BF16),
            pltpu.VMEM((4, NC, 2, rows, dc), BF16),
            pltpu.VMEM((4, NC, 2, rows, dc), BF16),
            pltpu.VMEM((NC, 2, rows, dc), BF16),
            pltpu.VMEM((4, 4, SLOTS, rows), BF16),
            pltpu.VMEM((4, 4, SLOTS, rows), BF16),
            pltpu.VMEM((4, 4, SLOTS, rows), BF16),
            pltpu.VMEM((4, 4, SLOTS, rows), BF16),
            pltpu.VMEM((4, SLOTS, rows), BF16),
            pltpu.VMEM((2, rows, rows), BF16),
            pltpu.VMEM((4, rows, rows), F32),
            pltpu.VMEM((rows, rows), F32),
            pltpu.VMEM((8, rows, rows), F32),
            pltpu.VMEM((8, rows, rows), BF16),
            pltpu.VMEM((4, 4, SLOTS, rows), BF16),
            pltpu.VMEM((3, rows, rows), BF16),
            pltpu.VMEM((4, 4, SLOTS, rows), BF16),
            pltpu.VMEM((NC, rows, dc), BF16),
            pltpu.VMEM((NC, rows, dc), BF16),
            dma((2, NC)),
            dma((2, NC)),
            dma((7, NC)),
            dma((4, NC)),
            dma((NC,)),
            dma((2, NC)),
            dma((3, NC)),
            dma((7, NC)),
            dma((3, NC)),
            dma((4, NC)),
            dma((3,)), dma((4,)),
            dma((3,)), dma((4,)),
            dma((4,)), dma((4,)),
            dma((3,)), dma((3,)),
            dma((4, 4)), dma((4, 4)),
        ],
        compiler_params=pltpu.CompilerParams(
            collective_id=0, has_side_effects=True, vmem_limit_bytes=60 * 1024 * 1024
        ),
    )(queries, passages, hard_index.T, weights.reshape(1, rows))
    return loss.reshape(rows), gq, gp


def solution(mesh):
    in_specs = (
        P(("grp", "blk"), None),
        P(("grp", "blk"), None),
        P(("grp", "blk"), None),
        P(("grp", "blk")),
    )
    out_specs = (P(("grp", "blk")), P(("grp", "blk"), None), P(("grp", "blk"), None))
    chunks = 16
    return jax.shard_map(
        functools.partial(per_device, chunks, mesh.shape["blk"] // 4),
        mesh=mesh, in_specs=in_specs, out_specs=out_specs, check_vma=False,
    )
```

time: 205 us -> 191 us (0.932)
  Pallas kernels: 194 us -> 186 us
  other arithmetic: 3.1 us -> 0 us
    pallas_call x1, Pallas kernels: 194 us -> 186 us  [per_device(): pl.pallas_call(functools.partial(kernel, NC, Y, cap), out_shape=(jax.Shap...]
    convert_element_type x3 -> x0, other arithmetic: 2.24 us -> none  [the longest x1 0.8 us: index_tiles(): (slot_row[:, :, None] == jnp.arange(rows)[None, None, :]).astype(BF16)]
    unnamed x11 -> x7, local copies, waits for them, and re-layouts: 5.56 us -> 4.43 us
where the time goes in v2:
time: 191 us
  Pallas kernels  186 us (97%)
  local copies, waits for them, and re-layouts  4.43 us (2%)
    pallas_call x1, Pallas kernels, per_device(): pl.pallas_call(functools.partial(kernel, NC, Y, cap), out_shape=(jax.Shap...  186 us
    unnamed x7, local copies, waits for them, and re-layouts  4.43 us

profile of v2, /device:TPU:1, one launch (start us, length us, event | category | flops | bytes accessed | tf_op | source)
XLA Modules:
  0.0 191.0 jit_solution(1066863266940857981)
XLA Ops:
  0.6 185.9 %shard_map.67 = (f32[1,128]{1,0:T(1,128)}, bf16[128,4096]{1,0:T(8,128)(2,1)}, bf16[128,4096]{1,0:T(8,128)(2,1)}) custom-call(bf16[128,4096]{1,0:T(8,128)(2,1)} %q_hbm.1, bf16[128,4096]{1,0:T(8,128)(2,1)} %p_hbm.1, s32[3,128]{1,0:T(4,128)} %bitcast.3, f32[1,128]{1,0:T(1,128)} %bitcast.4), custom_call_target="tpu_custom_call" | custom-call | tf_op jit(solution)/shard_map/pallas_call | solution.py:410
  186.6 0.0 copy-start.1
  186.6 0.6 copy-done.1
  187.1 0.5 copy.10
  187.6 0.0 copy-start
  187.6 2.4 %copy.11 = bf16[128,4096]{1,0:T(8,128)(2,1)} copy(bf16[128,4096]{1,0:T(8,128)(2,1)} %get-tuple-element.13) | data formatting | bytes 2097152
  190.0 0.0 copy-done
  190.0 1.0 copy.12
Async XLA Ops:
  186.6 0.6 copy-start.1
  187.6 2.4 %copy-start = (bf16[128,4096]{1,0:T(8,128)(2,1)S(1)}, bf16[128,4096]{1,0:T(8,128)(2,1)}, u32[]{:S(2)}) copy-start(bf16[128,4096]{1,0:T(8,128)(2,1)} %get-tuple-element.14) | copy-start | bytes 3145732

commit v3 on v2

--- a/solution.py
+++ b/solution.py
@@ -10,7 +10,8 @@
 MESH = pl.DeviceIdType.MESH
 TEMP = 50.0
 SLOTS = 32
-LAG = 4
+AHEAD = 1
+LAG_HOP2, LAG_HOP3, LAG_OUT, LAG_WIN, LAG_PICK, LAG_SCORE = 1, 1, 1, 2, 1, 4
 NEG = -3.0e38
 F32, BF16 = jnp.float32, jnp.bfloat16
 
@@ -153,8 +154,8 @@
                 z_s.at[1, cc], col_r.at[p, cc], z_out,
             ).start()
 
-    own(0)
-    own(1)
+    for k in range(AHEAD):
+        own(k)
 
     @pl.when(outer)
     def _():
@@ -183,8 +184,6 @@
         pk[0] = tn(unpack, rxo[...].reshape(rows, rows)).astype(BF16)
         pk[1] = tn(unpack, st[a(0)].reshape(rows, rows)).astype(BF16)
 
-    own_out(0)
-    own_out(1)
     for dx in (1, 2, 3):
         got(rx.at[:, (x + dx) % 4], rx_r.at[(x + dx) % 4])
         got(sc.at[(p + dx) % 4], sc_r.at[(p + dx) % 4])
@@ -203,7 +202,7 @@
         rcopy(src.at[0], bw.at[pi, cc], z_s.at[k, cc], bw_r.at[pi, cc], dev).start()
         rcopy(src.at[1], bw.at[qi, cc], z_s.at[k + 1, cc], bw_r.at[qi, cc], dev).start()
 
-    def hop12(cc):
+    def hop1(cc):
         @pl.when(outer)
         def _():
             got(col.at[a(2), cc], col_r.at[a(2), cc])
@@ -213,6 +212,10 @@
         def _():
             fwd_col(a(0), cc, 2, z_in)
             fwd_col(a(2), cc, 3, z_out)
+
+    def hop2(cc):
+        @pl.when(inner)
+        def _():
             fwd_col(a(3), cc, 4, z_out)
 
     def hop3(cc):
@@ -222,8 +225,6 @@
             to_win(col.at[a(3), cc], cc, 3, z_out, 1 - h)
             got(tr.at[cc], tr_r.at[cc])
             to_win(tr.at[cc], cc, 5, z_in, h)
-            part = col.at[a(1), cc, :, pl.ds(0, packed)]
-            got(part, col_r.at[a(1), cc])
 
     def win(cc):
         wi = 1 + 3 * h
@@ -238,6 +239,10 @@
             ).start()
 
     def pick_rows(cc):
+        @pl.when(outer)
+        def _():
+            got(col.at[a(1), cc, :, pl.ds(0, packed)], col_r.at[a(1), cc])
+
         for l in range(4):
             rows_p = nn(rx[l].reshape(4 * SLOTS, rows), col[l, cc, 0]).astype(BF16)
             xs[:, cc, 0, l * SLOTS : (l + 1) * SLOTS, :] = rows_p.reshape(4, SLOTS, dc)
@@ -261,34 +266,25 @@
             acc[5 + s] += nt(q, xr[(x + 1 + s) % 4, cc, 0])
 
     def step(t, carry):
-        @pl.when(t + 2 < NC)
-        def _():
-            own(t + 2)
-            own_out(t + 2)
-
-        @pl.when(t < NC)
-        def _():
-            hop12(t)
-
-        @pl.when((t >= 1) & (t < NC + 1))
-        def _():
-            hop3(t - 1)
-
-        @pl.when((t >= 2) & (t < NC + 2))
-        def _():
-            win(t - 2)
-
-        @pl.when((t >= 1) & (t < NC + 1))
-        def _():
-            pick_rows(t - 1)
-
-        @pl.when(t >= LAG)
-        def _():
-            score(t - LAG)
-
+        def stage(lag, part):
+            @pl.when((t >= lag) & (t < NC + lag))
+            def _():
+                part(t - lag)
+
+        @pl.when(t + AHEAD < NC)
+        def _():
+            own(t + AHEAD)
+
+        stage(0, hop1)
+        stage(LAG_HOP2, hop2)
+        stage(LAG_HOP3, hop3)
+        stage(LAG_OUT, own_out)
+        stage(LAG_WIN, win)
+        stage(LAG_PICK, pick_rows)
+        stage(LAG_SCORE, score)
         return carry
 
-    lax.fori_loop(0, NC + LAG, step, 0)
+    lax.fori_loop(0, NC + LAG_SCORE, step, 0)
 
     w = wm[...]
     scores = [TEMP * acc[k] for k in range(4)]

time: 191 us -> 185 us (0.969)
  Pallas kernels: 186 us -> 180 us
    pallas_call x1, Pallas kernels: 186 us -> 180 us  [per_device(): pl.pallas_call(functools.partial(kernel, NC, Y, cap), out_shape=(jax.Shap...]
where the time goes in v3:
time: 185 us
  Pallas kernels  180 us (97%)
  local copies, waits for them, and re-layouts  4.43 us (2%)
    pallas_call x1, Pallas kernels, per_device(): pl.pallas_call(functools.partial(kernel, NC, Y, cap), out_shape=(jax.Shap...  180 us
    unnamed x7, local copies, waits for them, and re-layouts  4.43 us

profile of v3, /device:TPU:1, one launch (start us, length us, event | category | flops | bytes accessed | tf_op | source)
XLA Modules:
  0.0 185.0 jit_solution(12895971171062158627)
XLA Ops:
  0.6 179.9 %shard_map.67 = (f32[1,128]{1,0:T(1,128)}, bf16[128,4096]{1,0:T(8,128)(2,1)}, bf16[128,4096]{1,0:T(8,128)(2,1)}) custom-call(bf16[128,4096]{1,0:T(8,128)(2,1)} %q_hbm.1, bf16[128,4096]{1,0:T(8,128)(2,1)} %p_hbm.1, s32[3,128]{1,0:T(4,128)} %bitcast.3, f32[1,128]{1,0:T(1,128)} %bitcast.4), custom_call_target="tpu_custom_call" | custom-call | tf_op jit(solution)/shard_map/pallas_call | solution.py:406
  180.5 0.0 copy-start.1
  180.5 0.6 copy-done.1
  181.1 0.5 copy.10
  181.6 0.0 copy-start
  181.6 2.4 %copy.11 = bf16[128,4096]{1,0:T(8,128)(2,1)} copy(bf16[128,4096]{1,0:T(8,128)(2,1)} %get-tuple-element.13) | data formatting | bytes 2097152
  184.0 0.0 copy-done
  184.0 1.0 copy.12
Async XLA Ops:
  180.5 0.6 copy-start.1
  181.6 2.4 %copy-start = (bf16[128,4096]{1,0:T(8,128)(2,1)S(1)}, bf16[128,4096]{1,0:T(8,128)(2,1)}, u32[]{:S(2)}) copy-start(bf16[128,4096]{1,0:T(8,128)(2,1)} %get-tuple-element.14) | copy-start | bytes 3145732

commit v4 on v3

--- a/solution.py
+++ b/solution.py
@@ -11,7 +11,7 @@
 TEMP = 50.0
 SLOTS = 32
 AHEAD = 1
-LAG_HOP2, LAG_HOP3, LAG_OUT, LAG_WIN, LAG_PICK, LAG_SCORE = 1, 1, 1, 2, 1, 4
+LAG_HOP2, LAG_HOP3, LAG_OUT, LAG_WIN, LAG_PICK, LAG_SCORE = 1, 1, 0, 2, 1, 3
 NEG = -3.0e38
 F32, BF16 = jnp.float32, jnp.bfloat16
 
@@ -30,8 +30,8 @@
 
 def kernel(
     NC, Y, CAP, q_hbm, p_hbm, hidx, wrow, loss, gq_hbm, gp_hbm,
-    col, bw, tr, xs, xr, ob, rt, st, rx, sc, rxo, pk, mx, wm, acc, wts, mts, wtw, mtx, oq, op,
-    ld_s, st_s, z_s, col_r, tr_r, own_s, win_s, bw_r, x_s, x_r,
+    col, bw, xs, xr, ob, rt, st, rx, sc, rxo, pk, mx, wm, acc, wts, mts, wtw, mtx, oq, op,
+    ld_s, st_s, z_s, col_r, own_s, win_s, bw_r, x_s, x_r,
     rx_s, rx_r, sc_s, sc_r, ro_s, ro_r, ww_s, ww_r, mt_s, mt_r,
 ):
     rows = 128
@@ -63,7 +63,7 @@
     def xdev(xx, pp):
         return (pp * 4 + xx, b)
 
-    z_in, z_out = zdev(z + 1 - 2 * m), zdev(z - 1 + 2 * m)
+    z_in, z_out, z_far = zdev(z + 1 - 2 * m), zdev(z - 1 + 2 * m), zdev(z - 2 + 4 * m)
 
     def rcopy(src, dst, ssem, rsem, dev):
         return pltpu.make_async_remote_copy(
@@ -87,6 +87,8 @@
         hello(bdev(off))
         hello(bdev(-off))
     hello(bdev(5 - 10 * c))
+
+    hello(z_far)
 
     @pl.when(outer)
     def _():
@@ -133,7 +135,7 @@
 
         lax.fori_loop(0, NC, clear, 0)
 
-    pl.semaphore_wait(barrier, 25 - ((p + 1) // 2) % 2)
+    pl.semaphore_wait(barrier, 26 - ((p + 1) // 2) % 2)
 
     def own(cc):
         load(p_hbm, 0, cc).wait()
@@ -206,7 +208,7 @@
         @pl.when(outer)
         def _():
             got(col.at[a(2), cc], col_r.at[a(2), cc])
-            rcopy(col.at[a(2), cc], tr.at[cc], z_s.at[2, cc], tr_r.at[cc], z_out).start()
+            to_win(col.at[a(2), cc], cc, 5, z_far, 1 - h)
 
         @pl.when(inner)
         def _():
@@ -223,8 +225,6 @@
         def _():
             got(col.at[a(3), cc], col_r.at[a(3), cc])
             to_win(col.at[a(3), cc], cc, 3, z_out, 1 - h)
-            got(tr.at[cc], tr_r.at[cc])
-            to_win(tr.at[cc], cc, 5, z_in, h)
 
     def win(cc):
         wi = 1 + 3 * h
@@ -362,7 +362,6 @@
         sent(col.at[p, cc], z_s.at[0, cc])
         sent(col.at[p, cc, 0], own_s.at[0, cc])
         sent(col.at[p, cc, 1], own_s.at[1, cc])
-        sent(col.at[p, cc], z_s.at[2, cc])
         for k in range(3):
             sent(bw.at[6, cc], win_s.at[k, cc])
             sent(xs.at[0, cc], x_s.at[k, cc])
@@ -375,7 +374,7 @@
         @pl.when(inner)
         def _():
             sent(ob.at[cc, :, pl.ds(0, packed)], z_s.at[1, cc])
-            for k in (3, 4):
+            for k in (2, 3, 4):
                 sent(col.at[p, cc], z_s.at[k, cc])
 
         return carry
@@ -415,7 +414,6 @@
         scratch_shapes=[
             pltpu.VMEM((4, NC, 2, rows, dc), BF16),
             pltpu.VMEM((7, NC, rows, dc), BF16),
-            pltpu.VMEM((NC, 2, rows, dc), BF16),
             pltpu.VMEM((4, NC, 2, rows, dc), BF16),
             pltpu.VMEM((4, NC, 2, rows, dc), BF16),
             pltpu.VMEM((NC, 2, rows, dc), BF16),
@@ -438,7 +436,6 @@
             dma((2, NC)),
             dma((7, NC)),
             dma((4, NC)),
-            dma((NC,)),
             dma((2, NC)),
             dma((3, NC)),
             dma((7, NC)),

time: 185 us -> 184 us (level)
  no operation moved by 1% of the time
where the time goes in v4:
time: 184 us
  Pallas kernels  179 us (97%)
  local copies, waits for them, and re-layouts  4.43 us (2%)
    pallas_call x1, Pallas kernels, per_device(): pl.pallas_call(functools.partial(kernel, NC, Y, cap), out_shape=(jax.Shap...  179 us
    unnamed x7, local copies, waits for them, and re-layouts  4.43 us

profile of v4, /device:TPU:1, one launch (start us, length us, event | category | flops | bytes accessed | tf_op | source)
XLA Modules:
  0.0 184.3 jit_solution(12315555624781107434)
XLA Ops:
  0.6 179.2 %shard_map.67 = (f32[1,128]{1,0:T(1,128)}, bf16[128,4096]{1,0:T(8,128)(2,1)}, bf16[128,4096]{1,0:T(8,128)(2,1)}) custom-call(bf16[128,4096]{1,0:T(8,128)(2,1)} %q_hbm.1, bf16[128,4096]{1,0:T(8,128)(2,1)} %p_hbm.1, s32[3,128]{1,0:T(4,128)} %bitcast.3, f32[1,128]{1,0:T(1,128)} %bitcast.4), custom_call_target="tpu_custom_call" | custom-call | tf_op jit(solution)/shard_map/pallas_call | solution.py:405
  179.9 0.0 copy-start.1
  179.9 0.6 copy-done.1
  180.4 0.5 copy.10
  180.9 0.0 copy-start
  180.9 2.4 %copy.11 = bf16[128,4096]{1,0:T(8,128)(2,1)} copy(bf16[128,4096]{1,0:T(8,128)(2,1)} %get-tuple-element.13) | data formatting | bytes 2097152
  183.3 0.0 copy-done
  183.3 1.0 copy.12
Async XLA Ops:
  179.9 0.6 copy-start.1
  180.9 2.4 %copy-start = (bf16[128,4096]{1,0:T(8,128)(2,1)S(1)}, bf16[128,4096]{1,0:T(8,128)(2,1)}, u32[]{:S(2)}) copy-start(bf16[128,4096]{1,0:T(8,128)(2,1)} %get-tuple-element.14) | copy-start | bytes 3145732
